TPU v7x, 32 devices: a whole 2x2x4 slice. The times are simulated.
32 devices in a mesh: range: 4 (over y, core), chan: 8 (over z, x).
Axes of the slice: x: 2, y: 2, z: 4, core: 2. Of those that a mesh axis runs over, the one named last changes fastest.
Arguments:
- echoes: float32 [2, 64, 512, 1024], P(None, 'chan', None, 'range'), may hold values from -18 to 18
- chirp: float32 [2, 129], replicated, may hold values from -0.375 to 0.375
- train_mask: int32 [512, 8], P('chan', 'range'), may hold values from 0 to 1, as said below
Outputs:
- spectra: bfloat16 [2, 512, 64, 1024], P(None, 'chan', None, 'range')
- factors: float32 [512, 2, 128, 128], P('chan')
Inputs may be any that keep to these rules, and one draw needn't show every extreme that they name: `train_mask`: in each Doppler bin exactly 4 consecutive tiles are 0 and all other tiles are 1.
All inputs are finite; a program needn't handle non-finite values.
Results may differ from a plain program's by a relative error of at most 0.001.
Values sent between devices are 32-bit elements; how exact they have to be, the bound alone decides.
A program may use at most 128 MiB of HBM per device.

v0:
```python
import math

import jax
import jax.numpy as jnp
from jax import lax
from jax.sharding import PartitionSpec as P

TILE = 128


best_precision = lax.Precision.HIGHEST


def from_behind(value, axis, steps):
    count = lax.axis_size(axis)
    leading, last = (max(0, -steps), min(count, count - steps))
    return lax.ppermute(value, axis, [(source, source + steps) for source in range(leading, last)])


def from_behind_2(block, axis, distance):
    devices = range(lax.axis_size(axis))
    route = [((i - distance) % len(devices), i) for i in devices]
    return lax.ppermute(block, axis, route)


def toeplitz_rows(taps):
    tap_span = taps.shape[-1] - 1
    padded = jnp.concatenate([taps, jnp.zeros((taps.shape[0], tap_span), taps.dtype)], -1)
    tiled = jnp.tile(padded, (1, tap_span))
    return tiled[:, : 2 * tap_span * tap_span].reshape(taps.shape[0], tap_span, 2 * tap_span)


def compress(extended, taps):
    tap_span = taps.shape[-1] - 1
    lead_shape = extended.shape[:-1]
    block_count = extended.shape[-1] // tap_span - 1
    blocks = extended.reshape(lead_shape + (block_count + 1, tap_span))
    window = jnp.concatenate([blocks[..., :block_count, :], blocks[..., 1:, :]], -1)
    kernel = toeplitz_rows(taps)
    products = jnp.einsum(
        "tcpnk,sok->tscpno",
        window,
        kernel,
        precision=best_precision,
        preferred_element_type=jnp.float32,
    )
    real_part = products[0, 0] + products[1, 1]
    imag_part = products[1, 0] - products[0, 1]
    return jnp.stack([real_part, imag_part]).reshape(lead_shape + (block_count * tap_span,))


def doppler_table(bin_numbers, pulse_count):
    phase_index = (
        bin_numbers[:, None] * jnp.arange(pulse_count, dtype=jnp.int32)[None, :] % pulse_count
    )
    angles = phase_index.astype(jnp.float32) * (2.0 * math.pi / pulse_count)
    scaling = 1.0 / math.sqrt(pulse_count)
    return jnp.stack([jnp.cos(angles) * scaling, -jnp.sin(angles) * scaling])


def doppler(signal, dft_table):
    products = jnp.einsum(
        "sdp,tcpg->stdcg",
        dft_table,
        signal,
        precision=best_precision,
        preferred_element_type=jnp.float32,
    )
    return jnp.stack([products[0, 0] - products[1, 1], products[0, 1] + products[1, 0]])


def gram_block(spectra_now, spectra_next, weights, scaling):
    snapshot = jnp.concatenate([spectra_now, spectra_next], 2)
    masked = snapshot * weights[None, :, None, :]
    products = jnp.einsum(
        "tbkg,sblg->btskl",
        masked,
        snapshot,
        precision=best_precision,
        preferred_element_type=jnp.float32,
    )
    real_part = products[:, 0, 0] + products[:, 1, 1]
    imag_part = products[:, 0, 1] - products[:, 1, 0]
    return jnp.stack([real_part, imag_part], 1) * scaling


def factor(gram):
    order_size = gram.shape[-1]
    strip_size = min(16, order_size)
    columns = jnp.arange(order_size, dtype=jnp.int32)
    remaining = gram
    pieces = []
    for offset in range(0, order_size, strip_size):
        strip_rows = remaining[:, :, :strip_size, :]

        def column_step(position, carry):
            strip_now, found_rows = carry
            place = offset + position
            row_now = lax.dynamic_index_in_dim(strip_now, position, 2, keepdims=False)
            pivots = jnp.sum(jnp.where(columns == place, row_now[:, 0], 0.0), -1)
            inverse = lax.rsqrt(pivots)[:, None]
            row_real = jnp.where(columns >= place, row_now[:, 0] * inverse, 0.0)
            row_imag = jnp.where(columns > place, row_now[:, 1] * inverse, 0.0)
            coef_real = row_real[:, offset : offset + strip_size]
            coef_imag = row_imag[:, offset : offset + strip_size]
            new_real = (
                strip_now[:, 0]
                - coef_real[:, :, None] * row_real[:, None, :]
                - coef_imag[:, :, None] * row_imag[:, None, :]
            )
            new_imag = (
                strip_now[:, 1]
                - coef_real[:, :, None] * row_imag[:, None, :]
                + coef_imag[:, :, None] * row_real[:, None, :]
            )
            found_rows = lax.dynamic_update_index_in_dim(
                found_rows, jnp.stack([row_real, row_imag], 1), position, 2
            )
            return (jnp.stack([new_real, new_imag], 1), found_rows)

        strip_end, found_rows = lax.fori_loop(
            0, strip_size, column_step, (strip_rows, jnp.zeros_like(strip_rows))
        )
        pieces.append(found_rows)
        if offset + strip_size < order_size:
            tail_part = found_rows[:, :, :, offset + strip_size :]
            products = jnp.einsum(
                "nabi,ncbj->nacij",
                tail_part,
                found_rows,
                precision=best_precision,
                preferred_element_type=jnp.float32,
            )
            update_real = products[:, 0, 0] + products[:, 1, 1]
            update_imag = products[:, 0, 1] - products[:, 1, 0]
            remaining = remaining[:, :, strip_size:, :] - jnp.stack([update_real, update_imag], 1)
    return jnp.concatenate(pieces, 2)


def on_device(echoes, chirp, train_mask):
    tap_span = chirp.shape[-1] - 1
    pulses = echoes.shape[2]
    gate_count = echoes.shape[3]
    rim_gates = from_behind(echoes[..., :tap_span], "range", -1)
    compressed = compress(jnp.concatenate([echoes, rim_gates], -1), chirp)
    spectra_all = doppler(compressed, doppler_table(jnp.arange(pulses, dtype=jnp.int32), pulses))
    turned = lax.all_to_all(spectra_all, "chan", split_axis=1, concat_axis=2, tiled=True)
    edge_bin = from_behind_2(turned[:, :1], "chan", -1)
    following = jnp.concatenate([turned[:, 1:], edge_bin], 1)
    spectra_out = turned.astype(jnp.bfloat16)
    total_gates = gate_count * lax.axis_size("range")
    scaling = 1.0 / total_gates
    weights = jnp.broadcast_to(
        train_mask.astype(jnp.float32)[:, :, None], train_mask.shape + (TILE,)
    ).reshape(train_mask.shape[0], gate_count)
    partial_gram = lax.psum_scatter(
        gram_block(turned, following, weights, scaling), "range", scatter_dimension=0, tiled=True
    )
    factors = lax.all_gather(factor(partial_gram), "range", axis=0, tiled=True)
    return (spectra_out, factors)


def solution(mesh):
    return jax.shard_map(
        on_device,
        mesh=mesh,
        in_specs=(P(None, "chan", None, "range"), P(), P("chan", "range")),
        out_specs=(P(None, "chan", None, "range"), P("chan", None, None, None)),
        check_vma=False,
    )
```

profile of v0, /device:TPU:0, one launch (start us, length us, event | category | flops | bytes accessed | tf_op | source)
XLA Modules:
  0.0 662.4 jit_solution(18391180482651036311)
XLA Ops:
  7.2 8.7 %copy.189 = f32[2,8,512,256]{2,3,1,0:T(8,128)} copy(f32[2,8,512,256]{3,2,1,0:T(8,128)} %param.19) | data formatting | bytes 16777216 | tf_op args[0]
  15.9 4.8 slice.757
  20.7 1.3 collective-permute-start
  22.6 4.2 negate_multiply_fusion
  26.7 3.4 collective-permute-done
  30.1 5.9 pad_maximum_fusion.8
  36.0 7.0 %fusion.104 = (f32[2,8,512,2,128]{2,4,3,1,0:T(8,128)}, f32[2,8,512,2,128]{2,4,3,1,0:T(8,128)}) fusion(f32[2,8,512,3,128]{2,4,3,1,0:T(8,128)S(1)} %bitcast.399), kind=kLoop, calls=%fused_computation.288 | loop fusion | bytes 33554432 | tf_op jit(solution)/shard_map/slice | solution.py:38
  43.0 8.7 %copy.286 = f32[2,8,512,2,128]{4,2,3,1,0:T(8,128)} copy(f32[2,8,512,2,128]{2,4,3,1,0:T(8,128)} %get-tuple-element.1093) | data formatting | bytes 16777216
  51.7 8.7 %copy.285 = f32[2,8,512,2,128]{4,2,3,1,0:T(8,128)} copy(f32[2,8,512,2,128]{2,4,3,1,0:T(8,128)} %get-tuple-element.1092) | data formatting | bytes 16777216
  60.4 21.7 %fusion.55 = f32[2,2,8,512,2,128]{3,5,4,2,0,1:T(8,128)} fusion(f32[2,8,512,2,128]{4,2,3,1,0:T(8,128)} %copy.286, f32[2,8,512,2,128]{4,2,3,1,0:T(8,128)} %copy.285, f32[1,2,128,256]{3,1,2,0:T(2,128)S(1)} %bitcast.450), kind=kOutput, calls=%fused_computation.179 | convolution fusion | flops 12889096192 | bytes 33816576 | tf_op jit(solution)/shard_map/tcpnk,sok->tscpno/dot_general | solution.py:40
  82.2 10.2 %slice_add_fusion.1 = (f32[1,1,8,512,2,128]{3,5,4,2,0,1:T(8,128)S(1)}, f32[1,1,8,512,2,128]{3,5,4,2,0,1:T(8,128)}) fusion(f32[2,2,8,512,2,128]{3,5,4,2,0,1:T(8,128)} %fusion.55), kind=kLoop, calls=%fused_computation.194 | loop fusion | flops 2097152 | bytes 25165824 | tf_op jit(solution)/shard_map/add | solution.py:47
  92.4 31.8 %fusion.56 = f32[2,2,512,8,256]{2,4,0,3,1:T(8,128)S(1)} fusion(f32[1,8,512,256]{2,3,1,0:T(8,128)} %bitcast.409, f32[1,8,512,256]{2,3,1,0:T(8,128)S(1)} %bitcast.408, f32[1,512,512]{2,1,0:T(8,128)S(1)} %get-tuple-element.1118, f32[1,512,512]{2,1,0:T(8,128)S(1)} %get-tuple-element.1119), kind=kOutput, calls=%fused_computation.180 | convolution fusion | flops 25772425216 | bytes 27262976 | tf_op jit(solution)/shard_map/sdp,tcpg->stdcg/dot_general | solution.py:62
  124.2 1.0 fusion.60
  125.2 1.0 fusion.62
  126.3 4.4 pad_maximum_fusion.9
  130.6 10.3 %copy.194 = f32[2,512,8,256]{3,2,0,1:T(8,128)} copy(f32[2,512,8,256]{1,3,2,0:T(8,128)} %pad_maximum_fusion.9) | data formatting | bytes 16777216 | tf_op jit(solution)/shard_map/stack | solution.py:69
  141.0 177.9 %all_to_all.18 = f32[2,512,8,256]{3,2,0,1:T(8,128)S(1)} all-to-all(f32[2,512,8,256]{3,2,0,1:T(8,128)} %copy.194), channel_id=1, replica_groups=mesh['range'=4,'chan'=8] {'chan'}, dimensions={1} | all-to-all | bytes 16777216 | tf_op jit(solution)/shard_map/all_to_all | solution.py:147
  318.9 1.3 copy.366
  320.2 2.2 copy-done
  322.4 3.3 copy-done.1
  325.7 3.1 collective-permute-start.1
  329.0 7.6 %slice.768 = f32[2,63,64,256]{3,2,0,1:T(8,128)} slice(f32[2,64,64,256]{3,2,0,1:T(8,128)} %bitcast.402), slice={[0:2], [1:64], [0:64], [0:256]} | slice | bytes 16515072 | tf_op jit(solution)/shard_map/slice | solution.py:149
  336.7 27.3 %fusion.46 = f32[64,2,2,128,128]{3,4,1,2,0:T(8,128)} fusion(f32[2,1,64,256]{3,2,0,1:T(8,128)S(1)} %collective-permute-done.1, f32[2,63,64,256]{3,2,0,1:T(8,128)} %slice.768, f32[2,64,64,256]{3,2,0,1:T(8,128)} %bitcast.403, f32[64,256]{1,0:T(8,128)S(1)} %bitcast.452), kind=kOutput, calls=%fused_computation.169 | convolution fusion | flops 12905873408 | bytes 33619968 | tf_op jit(solution)/shard_map/tbkg,sblg->btskl/dot_general | solution.py:75
  364.0 4.2 fusion.57
  368.2 4.2 fusion.59
  372.5 1.6 maximum_multiply_fusion
  374.1 1.1 copy.280
  375.2 8.0 %copy.365 = f32[8,8,256,128]{3,1,2,0:T(8,128)} copy(f32[8,8,256,128]{3,2,1,0:T(8,128)S(1)} %bitcast.404) | data formatting | bytes 16777216
  383.3 82.1 %reduce-scatter.5.cloned.1.call-done = f32[16,32768]{1,0:T(8,128)} async-done(((f32[64,32768]{1,0:T(8,128)}), f32[16,32768]{1,0:T(8,128)}) %reduce-scatter.5.cloned.1.call-update) | async-done | bytes 2097168
  465.4 2.0 copy.300
  467.4 1.9 slice.775
  469.3 0.6 copy.200
  469.9 9.0 %while.136 = (s32[]{:T(128)}, f32[16,2,16,128]{3,2,1,0:T(8,128)S(1)}, f32[16,2,16,128]{3,0,1,2:T(8,128)S(1)}, s32[]{:T(128)}) while((s32[]{:T(128)}, f32[16,2,16,128]{3,2,1,0:T(8,128)S(1)}, f32[16,2,16,128]{3,0,1,2:T(8,128)S(1)}, s32[]{:T(128)}) %tuple.404), condition=%wide.region_3.4_spmd.clone.clone, body=%wide.region_1.3_spmd.clone.clone.sunk | while | flops 345458 | bytes 1227949 | solution.py:121
  478.9 0.9 fusion.110
  479.8 3.3 convolution_bitcast_fusion
  483.2 1.0 fusion.73
  484.3 1.7 copy.292
  486.0 1.9 maximum_subtract_fusion
  488.0 11.2 %while.137 = (s32[]{:T(128)}, f32[16,2,16,128]{3,2,1,0:T(8,128)S(1)}, f32[16,2,16,128]{3,0,1,2:T(8,128)S(1)}, s32[]{:T(128)}, s32[]{:T(128)}) while((s32[]{:T(128)}, f32[16,2,16,128]{3,2,1,0:T(8,128)S(1)}, f32[16,2,16,128]{3,0,1,2:T(8,128)S(1)}, s32[]{:T(128)}, s32[]{:T(128)}) %tuple.407), condition=%wide.region_6.7_spmd.clone.clone, body=%wide.region_4.6_spmd.clone.clone.sunk | while | flops 345459 | bytes 1228033 | solution.py:121
  499.2 0.9 fusion.109
  500.1 2.9 convolution_bitcast_fusion.1
  503.4 1.1 copy-done.3
  504.6 11.2 %while.138 = (s32[]{:T(128)}, f32[16,2,16,128]{3,2,1,0:T(8,128)S(1)}, f32[16,2,16,128]{3,0,1,2:T(8,128)S(1)}, s32[]{:T(128)}, s32[]{:T(128)}) while((s32[]{:T(128)}, f32[16,2,16,128]{3,2,1,0:T(8,128)S(1)}, f32[16,2,16,128]{3,0,1,2:T(8,128)S(1)}, s32[]{:T(128)}, s32[]{:T(128)}) %tuple.410), condition=%wide.region_9.10_spmd.clone.clone, body=%wide.region_7.9_spmd.clone.clone.sunk | while | flops 345459 | bytes 1228033 | solution.py:121
  515.8 0.9 fusion.108
  516.7 2.4 convolution_bitcast_fusion.2
  519.5 11.3 %while.139 = (s32[]{:T(128)}, f32[16,2,16,128]{3,2,1,0:T(8,128)S(1)}, f32[16,2,16,128]{3,0,1,2:T(8,128)S(1)}, s32[]{:T(128)}, s32[]{:T(128)}) while((s32[]{:T(128)}, f32[16,2,16,128]{3,2,1,0:T(8,128)S(1)}, f32[16,2,16,128]{3,0,1,2:T(8,128)S(1)}, s32[]{:T(128)}, s32[]{:T(128)}) %tuple.413), condition=%wide.region_12.13_spmd.clone.clone, body=%wide.region_10.12_spmd.clone.clone.sunk | while | flops 345459 | bytes 1228033 | solution.py:121
  530.9 0.9 fusion.107
  531.8 2.0 convolution_bitcast_fusion.3
  534.2 11.2 %while.140 = (s32[]{:T(128)}, f32[16,2,16,128]{3,2,1,0:T(8,128)S(1)}, f32[16,2,16,128]{3,0,1,2:T(8,128)S(1)}, s32[]{:T(128)}, s32[]{:T(128)}) while((s32[]{:T(128)}, f32[16,2,16,128]{3,2,1,0:T(8,128)S(1)}, f32[16,2,16,128]{3,0,1,2:T(8,128)S(1)}, s32[]{:T(128)}, s32[]{:T(128)}) %tuple.416), condition=%wide.region_15.16_spmd.clone.clone, body=%wide.region_13.15_spmd.clone.clone.sunk | while | flops 345459 | bytes 1228033 | solution.py:121
  545.4 0.9 fusion.106
  546.3 1.6 convolution_bitcast_fusion.4
  548.2 11.2 %while.141 = (s32[]{:T(128)}, f32[16,2,16,128]{3,2,1,0:T(8,128)S(1)}, f32[16,2,16,128]{3,0,1,2:T(8,128)S(1)}, s32[]{:T(128)}, s32[]{:T(128)}) while((s32[]{:T(128)}, f32[16,2,16,128]{3,2,1,0:T(8,128)S(1)}, f32[16,2,16,128]{3,0,1,2:T(8,128)S(1)}, s32[]{:T(128)}, s32[]{:T(128)}) %tuple.419), condition=%wide.region_18.19_spmd.clone.clone, body=%wide.region_16.18_spmd.clone.clone.sunk | while | flops 345459 | bytes 1228033 | solution.py:121
  559.4 0.9 fusion.105
  560.2 1.3 convolution_bitcast_fusion.5
  561.8 11.2 %while.142 = (s32[]{:T(128)}, f32[16,2,16,128]{3,2,1,0:T(8,128)S(1)}, f32[16,2,16,128]{3,0,1,2:T(8,128)S(1)}, s32[]{:T(128)}, s32[]{:T(128)}) while((s32[]{:T(128)}, f32[16,2,16,128]{3,2,1,0:T(8,128)S(1)}, f32[16,2,16,128]{3,0,1,2:T(8,128)S(1)}, s32[]{:T(128)}, s32[]{:T(128)}) %tuple.422), condition=%wide.region_21.22_spmd.clone.clone, body=%wide.region_19.21_spmd.clone.clone.sunk | while | flops 345459 | bytes 1228033 | solution.py:121
  573.0 0.6 copy.227
  573.6 0.9 copy_dynamic-update-slice_fusion
  574.5 0.7 convolution_bitcast_fusion.6
  575.3 13.0 %while.143 = (s32[]{:T(128)}, f32[16,2,16,128]{3,2,1,0:T(8,128)S(1)}, f32[16,2,16,128]{3,2,1,0:T(8,128)S(1)}, s32[]{:T(128)}, s32[]{:T(128)}, /*index=5*/s32[]{:T(128)}) while((s32[]{:T(128)}, f32[16,2,16,128]{3,2,1,0:T(8,128)S(1)}, f32[16,2,16,128]{3,2,1,0:T(8,128)S(1)}, s32[]{:T(128)}, s32[]{:T(128)}, ...), condition=%wide.region_24.25_spmd.clone.clone, body=%wide.region_22.24_spmd.clone.clone.sunk | while | flops 345459 | bytes 1293577 | solution.py:121
  588.3 0.7 constant_dynamic-update-slice_fusion
  589.0 4.0 copy.368
  593.1 2.3 copy.239
  595.4 52.1 %all-gather.2.cloned.1.call-done = f32[64,2,128,128]{3,2,1,0:T(8,128)} async-done(((f32[16,2,128,128]{3,2,1,0:T(8,128)}), f32[64,2,128,128]{3,2,1,0:T(8,128)}) %all-gather.2.cloned.1.call-update) | async-done | bytes 8388624 | tf_op jit(solution)/shard_map/all_gather | solution.py:159
  647.5 7.9 %copy.476 = f32[64,2,128,128]{3,2,1,0:T(8,128)} copy(f32[64,2,128,128]{3,2,1,0:T(8,128)} %all-gather.2.cloned.1.call-done) | data formatting | bytes 16777216
  (1726 shorter events, 82.1 us)
Async XLA Ops:
  7.2 458.2 %reduce-scatter.5.cloned.1.call-start = ((), (), s32[]{:S(2)}) async-start(), calls=%async_computation.3 | async-start | bytes 10485760
  15.9 6.1 copy-start.6
  20.7 9.4 %collective-permute-start = (f32[2,8,512,128]{2,3,1,0:T(8,128)}, f32[2,8,512,128]{2,3,1,0:T(8,128)}, u32[]{:S(2)}, u32[]{:S(2)}) collective-permute-start(f32[2,8,512,128]{2,3,1,0:T(8,128)} %slice.757), channel_id=1, source_target_pairs={{8,0},{16,8},{24,16},{9,1},{17,9},{25,17},{10,2},{18,10},{26,18},{... | collective-permute-start | bytes 12582920 | tf_op jit(solution)/shard_map/ppermute | solution.py:17
  22.6 13.5 %copy-start.5 = (f32[2,32896]{1,0:T(2,128)}, f32[2,32896]{1,0:T(2,128)S(1)}, u32[]{:S(2)}) copy-start(f32[2,32896]{1,0:T(2,128)S(1)} %tile.10) | copy-start | bytes 789508
  51.7 8.7 %slice-start = ((f32[2,32896]{1,0:T(2,128)}), f32[2,32768]{1,0:T(2,128)S(1)}, s32[]{:S(2)}) async-start(f32[2,32896]{1,0:T(2,128)} %copy-done.5), calls=%async_computation.4 | async-start | bytes 524288 | tf_op jit(solution)/shard_map/slice | solution.py:30
  318.9 3.5 copy-start
  318.9 9.9 %copy-start.7 = (s32[64,2]{0,1:T(2,128)S(1)}, s32[64,2]{0,1:T(2,128)}, u32[]{:S(2)}) copy-start(s32[64,2]{0,1:T(2,128)} %param.21) | copy-start | bytes 1540
  322.4 3.3 copy-start.1
  325.7 11.0 %collective-permute-start.1 = (f32[2,1,64,256]{3,2,0,1:T(8,128)S(1)}, f32[2,1,64,256]{3,2,0,1:T(8,128)S(1)}, u32[]{:S(2)}, u32[]{:S(2)}) collective-permute-start(f32[2,1,64,256]{3,2,0,1:T(8,128)S(1)} %slice.769), channel_id=1, source_target_pairs={{1,0},{2,1},{3,2},{4,3},{5,4},{6,5},{7,6},{0,7},{9,8},{10,9},{11,1... | collective-permute-start | bytes 393224 | tf_op jit(solution)/shard_map/ppermute | solution.py:23
  383.3 264.2 %all-gather.2.cloned.1.call-start = ((), (), s32[]{:S(2)}) async-start(), calls=%async_computation.2 | async-start | bytes 10485760 | tf_op jit(solution)/shard_map/all_gather | solution.py:159
  479.8 4.4 copy-start.2
  503.4 1.1 copy-start.3
  515.8 3.5 copy-start.4
Sparse Core Ops, SparseCore 0:
  383.4 81.9 reduce-scatter.4
  589.2 58.2 all-gather.1
where the time goes:
time: 668 us; the launch traced here: 662 us
  blocking collectives  178 us (27%)
  waiting for transfers between devices  138 us (21%)
  local copies, waits for them, and re-layouts  124 us (19%)
  other arithmetic  98.4 us (15%)
  matrix products  95.1 us (14%)
  between operations  14.8 us (2%)
  loops' own time  9.89 us (1%)
    all_to_all x1, blocking collectives, on_device(): lax.all_to_all(spectra_all, 'chan', split_axis=1, concat_axis=2, tiled=True)  178 us
    unnamed x3, waiting for transfers between devices  82.1 us
    unnamed x35, local copies, waits for them, and re-layouts  57.4 us
    all_gather x1, waiting for transfers between devices, on_device(): factors = lax.all_gather(factor(partial_gram), 'range', axis=0, tiled=True)  52.1 us
    dot_general x1, matrix products, doppler(): jnp.einsum('sdp,tcpg->stdcg', dft_table, signal, precision=best_precision...  31.8 us
    dot_general x1, matrix products, gram_block(): jnp.einsum('tbkg,sblg->btskl', masked, snapshot, precision=best_precision...  27.3 us
    dot_general x1, matrix products, compress(): jnp.einsum('tcpnk,sok->tscpno', window, kernel, precision=best_precision,...  21.7 us
    select_n x256, other arithmetic, column_step(): row_real = jnp.where(columns >= place, row_now[:, 0] * inverse, 0.0)  19 us
  transfers between devices with their start and end apart: 4, of which 3 were waited for; matrix products, arithmetic and copies ran while one was open for 3% of the time, Pallas kernels for 0%

commit v1 on v0

v1 whole, which is shorter than its diff:
```python
import functools
import math

import jax
import jax.numpy as jnp
from jax import lax
from jax.experimental import pallas as pl
from jax.experimental.pallas import tpu as pltpu
from jax.sharding import PartitionSpec as P

LANES = 128
STRIP = 16
BF = jnp.bfloat16
F32 = jnp.float32
VMEM_LIMIT = 60 * 1024 * 1024


def split(x):
    high = x.astype(BF)
    return high, (x - high.astype(F32)).astype(BF)


def split_table(x):
    high = lax.reduce_precision(x, 8, 7)
    return high.astype(BF), (x - high).astype(BF)


def dot(a, b, dims=((1,), (0,))):
    return lax.dot_general(a, b, (dims, ((), ())), preferred_element_type=F32)


def dot3(a, b, dims=((1,), (0,))):
    (ah, al), (bh, bl) = a, b
    return dot(ah, bh, dims) + (dot(ah, bl, dims) + dot(al, bh, dims))


def from_behind(value, axis, steps):
    count = lax.axis_size(axis)
    leading, last = (max(0, -steps), min(count, count - steps))
    return lax.ppermute(value, axis, [(s, s + steps) for s in range(leading, last)])


def from_behind_2(block, axis, distance):
    devices = range(lax.axis_size(axis))
    route = [((i - distance) % len(devices), i) for i in devices]
    return lax.ppermute(block, axis, route)


def toeplitz_rows(taps):
    tap_span = taps.shape[-1] - 1
    padded = jnp.concatenate([taps, jnp.zeros((taps.shape[0], tap_span), taps.dtype)], -1)
    tiled = jnp.tile(padded, (1, tap_span))
    return tiled[:, : 2 * tap_span * tap_span].reshape(taps.shape[0], tap_span, 2 * tap_span)


def doppler_table(pulses):
    bins = jnp.arange(pulses, dtype=jnp.int32)
    phase = bins[:, None] * bins[None, :] % pulses
    angles = phase.astype(F32) * (2.0 * math.pi / pulses)
    scaling = 1.0 / math.sqrt(pulses)
    return jnp.concatenate([jnp.cos(angles) * scaling, -jnp.sin(angles) * scaling])


def spectra_kernel(channels, pulses, tiles, e_ref, h_ref, kh_ref, kl_ref, th_ref, tl_ref, s_ref):
    channel = pl.program_id(0)
    kernel = (kh_ref[...], kl_ref[...])
    wide = [jnp.concatenate([e_ref[p, 0], h_ref[p, 0]], -1) for p in range(2)]
    for t in range(tiles):
        window = jnp.concatenate(
            [w[:, t * LANES : (t + 2) * LANES] for w in wide], -1
        )
        y = split(dot3(split(window), kernel))
        step = min(256, pulses)
        for b in range(0, pulses, step):
            re = dot3((th_ref[pl.ds(b, step), :], tl_ref[pl.ds(b, step), :]), y)
            im = dot3((th_ref[pl.ds(pulses + b, step), :], tl_ref[pl.ds(pulses + b, step), :]), y)
            rows = pl.ds(b * channels + channel, step, stride=channels)
            s_ref[0, t, rows, :] = re[:, :LANES] - im[:, LANES:]
            s_ref[1, t, rows, :] = re[:, LANES:] + im[:, :LANES]


def make_spectra(echoes, rim, chirp):
    _, channels, pulses, gates = echoes.shape
    tiles = gates // LANES
    rows = toeplitz_rows(chirp)
    kr, ki = rows[0].T, rows[1].T
    kernel = jnp.concatenate(
        [jnp.concatenate([kr, -ki], 1), jnp.concatenate([ki, kr], 1)], 0
    )
    kh, kl = split_table(kernel)
    th, tl = split_table(doppler_table(pulses))
    full = lambda a: pl.BlockSpec(a.shape, lambda c: (0,) * a.ndim, pipeline_mode=pl.Buffered(1))
    return pl.pallas_call(
        functools.partial(spectra_kernel, channels, pulses, tiles),
        grid=(channels,),
        in_specs=[
            pl.BlockSpec((2, 1, pulses, gates), lambda c: (0, c, 0, 0)),
            pl.BlockSpec((2, 1, pulses, LANES), lambda c: (0, c, 0, 0)),
            full(kh), full(kl), full(th), full(tl),
        ],
        out_specs=pl.BlockSpec((2, tiles, pulses * channels, LANES), lambda c: (0, 0, 0, 0)),
        out_shape=jax.ShapeDtypeStruct((2, tiles, pulses * channels, LANES), F32),
        compiler_params=pltpu.CompilerParams(vmem_limit_bytes=VMEM_LIMIT),
        name="spectra",
    )(echoes, rim, kh, kl, th, tl)


def gram_kernel(bins, channels, tiles, scaling, w_ref, r_ref, f_ref, z_ref, o_ref):
    first = pl.program_id(0) * bins
    order = 2 * channels
    rows = lax.broadcasted_iota(jnp.int32, (order, order), 0)
    cols = lax.broadcasted_iota(jnp.int32, (order, order), 1)
    upper = rows <= cols

    def parts(j, part, t):
        now = r_ref[part, t, j]
        after = r_ref[part, t, j + 1] if j + 1 < bins else f_ref[part, t, 0]
        return jnp.concatenate([now, after], 0)

    for j in range(bins):
        pieces = [[parts(j, part, t) for t in range(tiles)] for part in range(2)]
        whole = jnp.concatenate([jnp.concatenate(p, 1) for p in pieces], 0)
        masked = jnp.concatenate(
            [
                jnp.concatenate(
                    [pieces[part][t] * w_ref[first + j, t] for t in range(tiles)], 1
                )
                for part in range(2)
            ],
            0,
        )
        g = dot3(split(masked), split(whole), ((1,), (1,)))
        re = g[:order, :order] + g[order:, order:]
        im = g[:order, order:] - g[order:, :order]
        z_ref[j] = jnp.where(upper, re, im) * scaling
        for part in range(2):
            for t in range(tiles):
                o_ref[part, j, :, t * LANES : (t + 1) * LANES] = r_ref[part, t, j].astype(BF)


def make_gram(turned, firsts, weights, scaling, bins):
    _, tiles, total, channels, _ = turned.shape
    order = 2 * channels
    return pl.pallas_call(
        functools.partial(gram_kernel, bins, channels, tiles, scaling),
        grid=(total // bins,),
        in_specs=[
            pl.BlockSpec(memory_space=pltpu.SMEM),
            pl.BlockSpec((2, tiles, bins, channels, LANES), lambda i: (0, 0, i, 0, 0)),
            pl.BlockSpec((2, tiles, 1, channels, LANES), lambda i: (0, 0, i, 0, 0)),
        ],
        out_specs=[
            pl.BlockSpec((bins, order, order), lambda i: (i, 0, 0)),
            pl.BlockSpec((2, bins, channels, tiles * LANES), lambda i: (0, i, 0, 0)),
        ],
        out_shape=[
            jax.ShapeDtypeStruct((total, order, order), F32),
            jax.ShapeDtypeStruct((2, total, channels, tiles * LANES), BF),
        ],
        compiler_params=pltpu.CompilerParams(vmem_limit_bytes=VMEM_LIMIT),
        name="gram",
    )(weights, turned, firsts)


def factor_kernel(count, order, z_ref, o_ref, re_ref, im_ref, sr_ref, si_ref):
    rows = lax.broadcasted_iota(jnp.int32, (order, order), 0)
    cols = lax.broadcasted_iota(jnp.int32, (order, order), 1)
    lane = lax.broadcasted_iota(jnp.int32, (count, order), 1)

    @pl.loop(0, count)
    def _(b):
        z = z_ref[b]
        re_ref[b] = z
        im_ref[b] = jnp.where(rows < cols, -z.T, 0.0)

    for offset in range(0, order, STRIP):
        for b in range(count):
            sr_ref[pl.ds(b, STRIP, stride=count), :] = re_ref[b, offset : offset + STRIP, :]
            si_ref[pl.ds(b, STRIP, stride=count), :] = im_ref[b, offset : offset + STRIP, :]
        now_r = [sr_ref[i * count : (i + 1) * count, :] for i in range(STRIP)]
        now_i = [si_ref[i * count : (i + 1) * count, :] for i in range(STRIP)]
        for i in range(STRIP):
            k = offset + i
            pivot = jnp.broadcast_to(now_r[i][:, k : k + 1], (count, order))
            root = lax.rsqrt(pivot)
            row_r = jnp.where(lane >= k, now_r[i] * root, 0.0)
            row_i = jnp.where(lane > k, now_i[i] * root, 0.0)
            for j in range(i + 1, STRIP):
                m = offset + j
                cr = jnp.broadcast_to(row_r[:, m : m + 1], (count, order))
                ci = jnp.broadcast_to(row_i[:, m : m + 1], (count, order))
                now_r[j] = now_r[j] - cr * row_r - ci * row_i
                now_i[j] = now_i[j] - cr * row_i + ci * row_r
            sr_ref[i * count : (i + 1) * count, :] = row_r
            si_ref[i * count : (i + 1) * count, :] = row_i
        done = offset + STRIP

        for b in range(count):
            fr = sr_ref[pl.ds(b, STRIP, stride=count), :]
            fi = si_ref[pl.ds(b, STRIP, stride=count), :]
            o_ref[b, 0, offset:done, :] = fr
            o_ref[b, 1, offset:done, :] = fi
            if done < order:
                left = jnp.concatenate([fr, fi], 0)
                right = jnp.concatenate(
                    [jnp.concatenate([fr, fi], 0), jnp.concatenate([fi, -fr], 0)], 1
                )
                lh, ll = split(left)
                rh, rl = split(right)
                update = dot(
                    jnp.concatenate([lh, lh, ll], 0)[:, :],
                    jnp.concatenate([rh, rl, rh], 0),
                    ((0,), (0,)),
                )
                re_ref[b, done:, :] = re_ref[b, done:, :] - update[done:, :order]
                im_ref[b, done:, :] = im_ref[b, done:, :] - update[done:, order:]


def make_factor(gram):
    count, order, _ = gram.shape
    return pl.pallas_call(
        functools.partial(factor_kernel, count, order),
        out_shape=jax.ShapeDtypeStruct((count, 2, order, order), F32),
        scratch_shapes=[
            pltpu.VMEM((count, order, order), F32),
            pltpu.VMEM((count, order, order), F32),
            pltpu.VMEM((STRIP * count, order), F32),
            pltpu.VMEM((STRIP * count, order), F32),
        ],
        compiler_params=pltpu.CompilerParams(vmem_limit_bytes=VMEM_LIMIT),
        name="factor",
    )(gram)


def pack_factor(factors):
    order = factors.shape[-1]
    keep = jnp.arange(order)[:, None] <= jnp.arange(order)[None, :]
    return jnp.where(keep, factors[:, 0], jnp.swapaxes(factors[:, 1], 1, 2))


def unpack_kernel(p_ref, o_ref):
    order = p_ref.shape[-1]
    rows = lax.broadcasted_iota(jnp.int32, (order, order), 0)
    cols = lax.broadcasted_iota(jnp.int32, (order, order), 1)
    for b in range(p_ref.shape[0]):
        z = p_ref[b]
        o_ref[b, 0] = jnp.where(rows <= cols, z, 0.0)
        o_ref[b, 1] = jnp.where(rows < cols, z.T, 0.0)


def unpack_factor(packed):
    total, order, _ = packed.shape
    bins = math.gcd(total, 8)
    return pl.pallas_call(
        unpack_kernel,
        grid=(total // bins,),
        in_specs=[pl.BlockSpec((bins, order, order), lambda i: (i, 0, 0))],
        out_specs=pl.BlockSpec((bins, 2, order, order), lambda i: (i, 0, 0, 0)),
        out_shape=jax.ShapeDtypeStruct((total, 2, order, order), F32),
        name="unpack",
    )(packed)


def on_device(echoes, chirp, train_mask):
    tap_span = chirp.shape[-1] - 1
    _, channels, pulses, gates = echoes.shape
    tiles = gates // LANES
    rim = from_behind(echoes[..., :tap_span], "range", -1)
    spectra = make_spectra(echoes, rim, chirp)
    spectra = spectra.reshape(2, tiles, pulses, channels, LANES)
    turned = lax.all_to_all(spectra, "chan", split_axis=2, concat_axis=3, tiled=True)
    edge = from_behind_2(turned[:, :, :1], "chan", -1)
    bins = math.gcd(turned.shape[2], 8)
    firsts = jnp.concatenate([turned[:, :, bins::bins], edge], 2)
    scaling = 1.0 / (gates * lax.axis_size("range"))
    packed, spectra_out = make_gram(turned, firsts, train_mask.astype(F32), scaling, bins)
    share = lax.psum_scatter(packed, "range", scatter_dimension=0, tiled=True)
    mine = pack_factor(make_factor(share))
    factors = unpack_factor(lax.all_gather(mine, "range", axis=0, tiled=True))
    return (spectra_out, factors)


def solution(mesh):
    return jax.shard_map(
        on_device,
        mesh=mesh,
        in_specs=(P(None, "chan", None, "range"), P(), P("chan", "range")),
        out_specs=(P(None, "chan", None, "range"), P("chan", None, None, None)),
        check_vma=False,
    )
```

time: 668 us -> 409 us (0.61)
  local copies, waits for them, and re-layouts: 124 us -> 23.7 us
  matrix products: 95.1 us -> 0 us
  other arithmetic: 98.4 us -> 8.89 us
  Pallas kernels: 0 us -> 81.5 us
  waiting for transfers between devices: 138 us -> 97.1 us
  loops' own time: 9.89 us -> 0 us
    dot_general x10 -> x0, matrix products: 95.1 us -> none  [the longest x1 31.8 us: doppler(): jnp.einsum('sdp,tcpg->stdcg', dft_table, signal, precision=best_precision...]
    unnamed x3 -> x2, waiting for transfers between devices: 82.1 us -> 0.03 us
    pallas_call x0 -> x4, Pallas kernels: none -> 81.5 us  [the longest x1 34.9 us: make_spectra(): pl.pallas_call(functools.partial(spectra_kernel, channels, pulses, tiles)...]
    reduce_scatter x0 -> x1, waiting for transfers between devices: none -> 61.9 us  [on_device(): share = lax.psum_scatter(packed, 'range', scatter_dimension=0, tiled=True)]
    unnamed x35 -> x9, local copies, waits for them, and re-layouts: 57.4 us -> 4.96 us
    slice x237 -> x5, local copies, waits for them, and re-layouts: 38.2 us -> 9.01 us  [the longest x1 4.61 us: on_device(): rim = from_behind(echoes[..., :tap_span], 'range', -1)]
    sub x138 -> x0, other arithmetic: 25.9 us -> none  [the longest x128 17.9 us: column_step(): strip_now[:, 0] - coef_real[:, :, None] * row_real[:, None, :]]
    select_n x256 -> x1, other arithmetic: 19 us -> 1.09 us  [pack_factor(): return jnp.where(keep, factors[:, 0], jnp.swapaxes(factors[:, 1], 1, 2))]
  transfers between devices with their start and end apart: 4 -> 4, of which waited for: 3 -> 3; matrix products, arithmetic and copies ran while one was open for 3% -> 2% of each run, Pallas kernels for 0% -> 0%
where the time goes in v1:
time: 409 us; the launch traced here: 408 us
  blocking collectives  178 us (44%)
  waiting for transfers between devices  97.1 us (24%)
  Pallas kernels  81.5 us (20%)
  local copies, waits for them, and re-layouts  23.7 us (6%)
  between operations  14.2 us (3%)
  other arithmetic  8.89 us (2%)
  starting transfers between devices  4.79 us (1%)
    all_to_all x1, blocking collectives, on_device(): lax.all_to_all(spectra, 'chan', split_axis=2, concat_axis=3, tiled=True)  178 us
    reduce_scatter x1, waiting for transfers between devices, on_device(): share = lax.psum_scatter(packed, 'range', scatter_dimension=0, tiled=True)  61.9 us
    pallas_call x1, Pallas kernels, make_spectra(): pl.pallas_call(functools.partial(spectra_kernel, channels, pulses, tiles)...  34.9 us
    all_gather x1, waiting for transfers between devices, on_device(): factors = unpack_factor(lax.all_gather(mine, 'range', axis=0, tiled=True))  34.6 us
    pallas_call x1, Pallas kernels, make_factor(): pl.pallas_call(functools.partial(factor_kernel, count, order), out_shape=...  26 us
    pallas_call x1, Pallas kernels, make_gram(): pl.pallas_call(functools.partial(gram_kernel, bins, channels, tiles, scal...  12.7 us
  transfers between devices with their start and end apart: 4, of which 3 were waited for; matrix products, arithmetic and copies ran while one was open for 2% of the time, Pallas kernels for 0%

profile of v1, /device:TPU:0, one launch (start us, length us, event | category | flops | bytes accessed | tf_op | source)
XLA Modules:
  0.0 407.9 jit_solution(6859358473547918752)
XLA Ops:
  7.2 0.0 copy-start.2
  7.2 0.0 reduce-scatter.2.cloned.1.call-start
  7.2 4.6 %slice.26 = f32[2,8,512,128]{3,2,1,0:T(8,128)} slice(f32[2,8,512,256]{3,2,1,0:T(8,128)} %e_ref.1), slice={[0:2], [0:8], [0:512], [0:128]} | slice | bytes 8388608 | tf_op jit(solution)/shard_map/slice | solution.py:268
  11.8 1.3 collective-permute-start
  13.1 0.0 copy-done.2
  13.2 0.5 tile.10
  13.7 0.7 slice_reduce_fusion
  14.4 0.1 copy.23
  14.6 0.1 copy.22
  14.7 0.9 fusion.8
  15.6 4.2 %negate_multiply_fusion = (f32[512,512]{1,0:T(8,128)S(1)}, f32[512,512]{1,0:T(8,128)S(1)}) fusion(), kind=kLoop, calls=%fused_computation.14 | loop fusion | flops 4456448 | bytes 2097152 | tf_op jit(solution)/shard_map/mul | solution.py:61
  19.7 1.6 fusion
  21.4 0.0 collective-permute-done.h_ref
  21.4 34.9 %spectra.1 = f32[2,2,4096,128]{3,2,1,0:T(8,128)} custom-call(f32[2,8,512,256]{3,2,1,0:T(8,128)} %e_ref.1, f32[2,8,512,128]{3,2,1,0:T(8,128)} %collective-permute-done.h_ref, bf16[512,256]{1,0:T(8,128)(2,1)} %get-tuple-element.11.kh_ref, bf16[512,256]{1,0:T(8,128)(2,1)} %get-tuple-element.10.kl_ref, bf16[1024,512]{1,0:T(8,128)(2,1)} %get-tuple-element.9.th_ref, ...), custom_call_target="tpu_custom_call" | custom-call | tf_op jit(solution)/shard_map/spectra/pallas_call | solution.py:93
  56.3 4.6 %copy.24 = f32[2,2,512,8,128]{4,3,1,0,2:T(8,128)S(1)} copy(f32[2,2,512,8,128]{4,3,2,1,0:T(8,128)} %bitcast.21) | data formatting | bytes 16777216 | tf_op jit(solution)/shard_map/reshape | solution.py:270
  60.9 177.7 %all_to_all.18 = f32[2,2,512,8,128]{4,3,1,0,2:T(8,128)S(1)} all-to-all(f32[2,2,512,8,128]{4,3,1,0,2:T(8,128)S(1)} %copy.24), channel_id=1, replica_groups=mesh['range'=4,'chan'=8] {'chan'}, dimensions={2} | all-to-all | bytes 16777216 | tf_op jit(solution)/shard_map/all_to_all | solution.py:271
  238.6 0.0 copy-start.3
  238.6 1.2 copy.33
  239.8 0.0 copy-start
  239.8 3.4 copy-done
  243.2 3.2 collective-permute-start.1
  246.4 0.0 copy-done.3
  246.4 0.7 copy.27.w_ref
  247.1 1.3 slice.29
  248.4 0.5 collective-permute-done.1
  249.0 1.1 pad_maximum_fusion.1.f_ref
  250.0 12.7 %gram.1 = (f32[64,128,128]{2,1,0:T(8,128)}, bf16[2,64,64,256]{3,2,1,0:T(8,128)(2,1)}) custom-call(f32[64,2]{1,0:T(8,128)} %copy.27.w_ref, f32[2,2,64,64,128]{4,3,2,1,0:T(8,128)} %bitcast.20, f32[2,2,8,64,128]{4,3,2,1,0:T(8,128)} %pad_maximum_fusion.1.f_ref), custom_call_target="tpu_custom_call" | custom-call | tf_op jit(solution)/shard_map/gram/pallas_call | solution.py:144
  262.8 0.0 reduce-scatter.2.cloned.1.call-update
  262.8 0.2 all-gather.2.cloned.1.call-start
  263.1 61.9 %reduce-scatter.2.cloned.1.call-done.z_ref = f32[16,128,128]{2,1,0:T(8,128)} async-done(((f32[64,128,128]{2,1,0:T(8,128)}), f32[16,128,128]{2,1,0:T(8,128)}) %reduce-scatter.2.cloned.1.call-update) | async-done | bytes 1048592 | tf_op jit(solution)/shard_map/reduce_scatter | solution.py:277
  324.9 26.0 %factor.1 = f32[16,2,128,128]{3,2,1,0:T(8,128)} custom-call(f32[16,128,128]{2,1,0:T(8,128)} %reduce-scatter.2.cloned.1.call-done.z_ref), custom_call_target="tpu_custom_call" | custom-call | tf_op jit(solution)/shard_map/factor/pallas_call | solution.py:221
  351.0 0.0 copy-start.1
  351.0 2.4 slice.36
  353.4 1.6 copy.31
  355.0 0.0 copy-done.1
  355.0 1.1 fusion.4
  356.1 2.5 copy.29
  358.6 0.0 all-gather.2.cloned.1.call-update
  358.6 34.6 %all-gather.2.cloned.1.call-done.p_ref = f32[64,128,128]{2,1,0:T(8,128)} async-done(((f32[16,128,128]{2,1,0:T(8,128)}), f32[64,128,128]{2,1,0:T(8,128)}) %all-gather.2.cloned.1.call-update) | async-done | bytes 4194320 | tf_op jit(solution)/shard_map/all_gather | solution.py:279
  393.3 7.8 %unpack.1 = f32[64,2,128,128]{3,2,1,0:T(8,128)} custom-call(f32[64,128,128]{2,1,0:T(8,128)} %all-gather.2.cloned.1.call-done.p_ref), custom_call_target="tpu_custom_call" | custom-call | tf_op jit(solution)/shard_map/unpack/pallas_call | solution.py:254
  (8 shorter events, 0.2 us)
Async XLA Ops:
  7.2 6.0 %copy-start.2 = (f32[2,129]{1,0:T(2,128)S(1)}, f32[2,129]{1,0:T(2,128)}, u32[]{:S(2)}) copy-start(f32[2,129]{1,0:T(2,128)} %param.4) | copy-start | bytes 3100
  7.2 317.8 %reduce-scatter.2.cloned.1.call-start = ((), (), s32[]{:S(2)}) async-start(), calls=%async_computation.2 | async-start | bytes 5242880 | tf_op jit(solution)/shard_map/reduce_scatter | solution.py:277
  11.8 9.5 %collective-permute-start = (f32[2,8,512,128]{3,2,1,0:T(8,128)}, f32[2,8,512,128]{3,2,1,0:T(8,128)}, u32[]{:S(2)}, u32[]{:S(2)}) collective-permute-start(f32[2,8,512,128]{3,2,1,0:T(8,128)} %slice.26), channel_id=1, source_target_pairs={{8,0},{16,8},{24,16},{9,1},{17,9},{25,17},{10,2},{18,10},{26,18},{... | collective-permute-start | bytes 12582920 | tf_op jit(solution)/shard_map/ppermute | solution.py:40
  238.6 7.9 %copy-start.3 = (s32[64,2]{0,1:T(2,128)S(1)}, s32[64,2]{0,1:T(2,128)}, u32[]{:S(2)}) copy-start(s32[64,2]{0,1:T(2,128)} %param.5) | copy-start | bytes 1540
  239.8 3.4 copy-start
  243.2 5.8 %collective-permute-start.1 = (f32[2,2,1,64,128]{4,3,2,1,0:T(8,128)S(1)}, f32[2,2,1,64,128]{4,3,2,1,0:T(8,128)S(1)}, u32[]{:S(2)}, u32[]{:S(2)}) collective-permute-start(f32[2,2,1,64,128]{4,3,2,1,0:T(8,128)S(1)} %slice.35), channel_id=1, source_target_pairs={{1,0},{2,1},{3,2},{4,3},{5,4},{6,5},{7,6},{0,7},{9,8},{10,9},{11,1... | collective-permute-start | bytes 393224 | tf_op jit(solution)/shard_map/ppermute | solution.py:46
  262.8 130.5 %all-gather.2.cloned.1.call-start = ((), (), s32[]{:S(2)}) async-start(), calls=%async_computation.3 | async-start | bytes 5242880 | tf_op jit(solution)/shard_map/all_gather | solution.py:279
  351.0 4.0 copy-start.1
Sparse Core Ops, SparseCore 0:
  262.9 61.9 reduce-scatter.1
  358.8 34.4 all-gather.1

commit v2 on v1

--- a/solution.py
+++ b/solution.py
@@ -10,6 +10,7 @@
 
 LANES = 128
 STRIP = 16
+CHUNKS = 4
 BF = jnp.bfloat16
 F32 = jnp.float32
 VMEM_LIMIT = 60 * 1024 * 1024
@@ -61,7 +62,7 @@
     return jnp.concatenate([jnp.cos(angles) * scaling, -jnp.sin(angles) * scaling])
 
 
-def spectra_kernel(channels, pulses, tiles, e_ref, h_ref, kh_ref, kl_ref, th_ref, tl_ref, s_ref):
+def spectra_kernel(channels, pulses, tiles, wrap, e_ref, h_ref, kh_ref, kl_ref, th_ref, tl_ref, s_ref):
     channel = pl.program_id(0)
     kernel = (kh_ref[...], kl_ref[...])
     wide = [jnp.concatenate([e_ref[p, 0], h_ref[p, 0]], -1) for p in range(2)]
@@ -75,11 +76,16 @@
             re = dot3((th_ref[pl.ds(b, step), :], tl_ref[pl.ds(b, step), :]), y)
             im = dot3((th_ref[pl.ds(pulses + b, step), :], tl_ref[pl.ds(pulses + b, step), :]), y)
             rows = pl.ds(b * channels + channel, step, stride=channels)
-            s_ref[0, t, rows, :] = re[:, :LANES] - im[:, LANES:]
-            s_ref[1, t, rows, :] = re[:, LANES:] + im[:, :LANES]
-
-
-def make_spectra(echoes, rim, chirp):
+            real = re[:, :LANES] - im[:, LANES:]
+            imag = re[:, LANES:] + im[:, :LANES]
+            s_ref[0, t, rows, :] = real
+            s_ref[1, t, rows, :] = imag
+            if wrap and b == 0:
+                s_ref[0, t, pl.ds(pulses * channels + channel, 1), :] = real[:1]
+                s_ref[1, t, pl.ds(pulses * channels + channel, 1), :] = imag[:1]
+
+
+def make_spectra(echoes, rim, chirp, wrap):
     _, channels, pulses, gates = echoes.shape
     tiles = gates // LANES
     rows = toeplitz_rows(chirp)
@@ -91,15 +97,15 @@
     th, tl = split_table(doppler_table(pulses))
     full = lambda a: pl.BlockSpec(a.shape, lambda c: (0,) * a.ndim, pipeline_mode=pl.Buffered(1))
     return pl.pallas_call(
-        functools.partial(spectra_kernel, channels, pulses, tiles),
+        functools.partial(spectra_kernel, channels, pulses, tiles, wrap),
         grid=(channels,),
         in_specs=[
             pl.BlockSpec((2, 1, pulses, gates), lambda c: (0, c, 0, 0)),
             pl.BlockSpec((2, 1, pulses, LANES), lambda c: (0, c, 0, 0)),
             full(kh), full(kl), full(th), full(tl),
         ],
-        out_specs=pl.BlockSpec((2, tiles, pulses * channels, LANES), lambda c: (0, 0, 0, 0)),
-        out_shape=jax.ShapeDtypeStruct((2, tiles, pulses * channels, LANES), F32),
+        out_specs=pl.BlockSpec((2, tiles, (pulses + wrap) * channels, LANES), lambda c: (0, 0, 0, 0)),
+        out_shape=jax.ShapeDtypeStruct((2, tiles, (pulses + wrap) * channels, LANES), F32),
         compiler_params=pltpu.CompilerParams(vmem_limit_bytes=VMEM_LIMIT),
         name="spectra",
     )(echoes, rim, kh, kl, th, tl)
@@ -160,6 +166,171 @@
         compiler_params=pltpu.CompilerParams(vmem_limit_bytes=VMEM_LIMIT),
         name="gram",
     )(weights, turned, firsts)
+
+
+def exchange_kernel(
+    chunk, scaling, w_ref, s_ref, share_ref, o_ref,
+    r_ref, z_ref, got_ref, own_sem, send_sem, recv_sem, zsend_sem, zrecv_sem,
+):
+    owners, ranges = lax.axis_size("chan"), lax.axis_size("range")
+    me, here = lax.axis_index("chan"), lax.axis_index("range")
+    _, tiles, _, channels, _ = s_ref.shape
+    total = o_ref.shape[1]
+    order = share_ref.shape[-1]
+    count = total // chunk
+    part = chunk // ranges
+
+    def chan_peer(k):
+        return {"chan": lax.rem(me + k, owners)}
+
+    def range_peer(k):
+        return {"range": lax.rem(here + k, ranges)}
+
+    barrier = pltpu.get_barrier_semaphore()
+    for k in range(1, owners):
+        pl.semaphore_signal(
+            barrier, inc=1, device_id=chan_peer(k), device_id_type=pl.DeviceIdType.MESH
+        )
+    for k in range(1, ranges):
+        pl.semaphore_signal(
+            barrier, inc=1, device_id=range_peer(k), device_id_type=pl.DeviceIdType.MESH
+        )
+    pl.semaphore_wait(barrier, owners + ranges - 2)
+
+    def span(c):
+        return (0, chunk + 1) if c == 0 else (c * chunk + 1, chunk)
+
+    mine = pl.ds(pl.multiple_of(me * channels, channels), channels)
+
+    def outgoing(c, k):
+        start, size = span(c)
+        owner = lax.rem(me + k, owners)
+        return pltpu.make_async_remote_copy(
+            src_ref=s_ref.at[:, :, pl.ds(owner * total + start, size)],
+            dst_ref=r_ref.at[:, :, pl.ds(start, size), mine],
+            send_sem=send_sem.at[c, k - 1],
+            recv_sem=recv_sem.at[c, k - 1],
+            device_id=chan_peer(k),
+            device_id_type=pl.DeviceIdType.MESH,
+        )
+
+    def local(c):
+        start, size = span(c)
+        return pltpu.make_async_copy(
+            s_ref.at[:, :, pl.ds(me * total + start, size)],
+            r_ref.at[:, :, pl.ds(start, size), mine],
+            own_sem.at[c],
+        )
+
+    def summand(c, k):
+        target = lax.rem(here + k, ranges)
+        return pltpu.make_async_remote_copy(
+            src_ref=z_ref.at[pl.ds(c * chunk + target * part, part)],
+            dst_ref=got_ref.at[c, k - 1],
+            send_sem=zsend_sem.at[c, k - 1],
+            recv_sem=zrecv_sem.at[c, k - 1],
+            device_id=range_peer(k),
+            device_id_type=pl.DeviceIdType.MESH,
+        )
+
+    for c in range(count):
+        for k in range(1, owners):
+            outgoing(c, k).start()
+        local(c).start()
+
+    rows = lax.broadcasted_iota(jnp.int32, (order, order), 0)
+    cols = lax.broadcasted_iota(jnp.int32, (order, order), 1)
+    upper = rows <= cols
+
+    def collect(c):
+        for k in range(1, ranges):
+            summand(c, k).wait_recv()
+
+        @pl.loop(0, part)
+        def _(j):
+            value = z_ref[c * chunk + here * part + j]
+            for k in range(1, ranges):
+                value = value + got_ref[c, k - 1, j]
+            share_ref[c * part + j] = value
+
+    for c in range(count):
+        for k in range(1, owners):
+            outgoing(c, k).wait_recv()
+        local(c).wait()
+
+        @pl.loop(0, chunk)
+        def _(i):
+            j = c * chunk + i
+            pieces = [
+                [r_ref[p, t, pl.ds(j, 2)].reshape(order, LANES) for t in range(tiles)]
+                for p in range(2)
+            ]
+            whole = jnp.concatenate([jnp.concatenate(p, 1) for p in pieces], 0)
+            masked = jnp.concatenate(
+                [
+                    jnp.concatenate([pieces[p][t] * w_ref[j, t] for t in range(tiles)], 1)
+                    for p in range(2)
+                ],
+                0,
+            )
+            g = dot3(split(masked), split(whole), ((1,), (1,)))
+            re = g[:order, :order] + g[order:, order:]
+            im = g[:order, order:] - g[order:, :order]
+            z_ref[j] = jnp.where(upper, re, im) * scaling
+
+        @pl.loop(0, chunk)
+        def _(i):
+            j = c * chunk + i
+            for p in range(2):
+                for t in range(tiles):
+                    o_ref[p, j, :, t * LANES : (t + 1) * LANES] = r_ref[p, t, j].astype(BF)
+
+        for k in range(1, ranges):
+            summand(c, k).start()
+        if c > 0:
+            collect(c - 1)
+    collect(count - 1)
+    for c in range(count):
+        for k in range(1, owners):
+            outgoing(c, k).wait_send()
+        for k in range(1, ranges):
+            summand(c, k).wait_send()
+
+
+def exchange(spectra, weights, scaling, chunk, owners, ranges):
+    _, tiles, _, channels, _ = spectra.shape
+    total = weights.shape[0]
+    full = channels * owners
+    order = 2 * full
+    count = total // chunk
+    part = chunk // ranges
+    dma = pltpu.SemaphoreType.DMA
+    return pl.pallas_call(
+        functools.partial(exchange_kernel, chunk, scaling),
+        in_specs=[
+            pl.BlockSpec(memory_space=pltpu.SMEM),
+            pl.BlockSpec(memory_space=pl.ANY),
+        ],
+        out_specs=[pl.BlockSpec(memory_space=pltpu.VMEM)] * 2,
+        out_shape=[
+            jax.ShapeDtypeStruct((count * part, order, order), F32),
+            jax.ShapeDtypeStruct((2, total, full, tiles * LANES), BF),
+        ],
+        scratch_shapes=[
+            pltpu.VMEM((2, tiles, total + 1, full, LANES), F32),
+            pltpu.VMEM((total, order, order), F32),
+            pltpu.VMEM((count, ranges - 1, part, order, order), F32),
+            dma((count,)),
+            dma((count, owners - 1)),
+            dma((count, owners - 1)),
+            dma((count, ranges - 1)),
+            dma((count, ranges - 1)),
+        ],
+        compiler_params=pltpu.CompilerParams(
+            vmem_limit_bytes=VMEM_LIMIT, collective_id=0, has_side_effects=True
+        ),
+        name="exchange",
+    )(weights, spectra)
 
 
 def factor_kernel(count, order, z_ref, o_ref, re_ref, im_ref, sr_ref, si_ref):
@@ -248,15 +419,20 @@
         o_ref[b, 1] = jnp.where(rows < cols, z.T, 0.0)
 
 
-def unpack_factor(packed):
-    total, order, _ = packed.shape
-    bins = math.gcd(total, 8)
+def unpack_factor(packed, count):
+    ranges, share, order, _ = packed.shape
+    bins = share // count
+    packed = packed.reshape(ranges, count, bins, order, order)
     return pl.pallas_call(
         unpack_kernel,
-        grid=(total // bins,),
-        in_specs=[pl.BlockSpec((bins, order, order), lambda i: (i, 0, 0))],
-        out_specs=pl.BlockSpec((bins, 2, order, order), lambda i: (i, 0, 0, 0)),
-        out_shape=jax.ShapeDtypeStruct((total, 2, order, order), F32),
+        grid=(count, ranges),
+        in_specs=[
+            pl.BlockSpec((None, None, bins, order, order), lambda c, r: (r, c, 0, 0, 0))
+        ],
+        out_specs=pl.BlockSpec(
+            (bins, 2, order, order), lambda c, r: (c * ranges + r, 0, 0, 0)
+        ),
+        out_shape=jax.ShapeDtypeStruct((ranges * share, 2, order, order), F32),
         name="unpack",
     )(packed)
 
@@ -265,18 +441,28 @@
     tap_span = chirp.shape[-1] - 1
     _, channels, pulses, gates = echoes.shape
     tiles = gates // LANES
+    ranges, owners = lax.axis_size("range"), lax.axis_size("chan")
+    total = train_mask.shape[0]
+    chunk = total // CHUNKS
     rim = from_behind(echoes[..., :tap_span], "range", -1)
-    spectra = make_spectra(echoes, rim, chirp)
-    spectra = spectra.reshape(2, tiles, pulses, channels, LANES)
-    turned = lax.all_to_all(spectra, "chan", split_axis=2, concat_axis=3, tiled=True)
-    edge = from_behind_2(turned[:, :, :1], "chan", -1)
-    bins = math.gcd(turned.shape[2], 8)
-    firsts = jnp.concatenate([turned[:, :, bins::bins], edge], 2)
-    scaling = 1.0 / (gates * lax.axis_size("range"))
-    packed, spectra_out = make_gram(turned, firsts, train_mask.astype(F32), scaling, bins)
-    share = lax.psum_scatter(packed, "range", scatter_dimension=0, tiled=True)
+    weights = train_mask.astype(F32)
+    scaling = 1.0 / (gates * ranges)
+    wrap = int(channels % 8 == 0 and chunk % ranges == 0)
+    spectra = make_spectra(echoes, rim, chirp, wrap)
+    spectra = spectra.reshape(2, tiles, pulses + wrap, channels, LANES)
+    if wrap:
+        count = CHUNKS
+        share, spectra_out = exchange(spectra, weights, scaling, chunk, owners, ranges)
+    else:
+        count = 1
+        turned = lax.all_to_all(spectra, "chan", split_axis=2, concat_axis=3, tiled=True)
+        edge = from_behind_2(turned[:, :, :1], "chan", -1)
+        bins = math.gcd(total, 8)
+        firsts = jnp.concatenate([turned[:, :, bins::bins], edge], 2)
+        packed, spectra_out = make_gram(turned, firsts, weights, scaling, bins)
+        share = lax.psum_scatter(packed, "range", scatter_dimension=0, tiled=True)
     mine = pack_factor(make_factor(share))
-    factors = unpack_factor(lax.all_gather(mine, "range", axis=0, tiled=True))
+    factors = unpack_factor(lax.all_gather(mine, "range", axis=0), count)
     return (spectra_out, factors)
 
 

time: 409 us -> 397 us (0.971)
  Pallas kernels: 81.5 us -> 306 us
  blocking collectives: 178 us -> 0 us
  waiting for transfers between devices: 97.1 us -> 49.4 us
  local copies, waits for them, and re-layouts: 23.7 us -> 18.1 us
    pallas_call x3, Pallas kernels: 55.4 us -> 280 us  [the longest x1 233 us: exchange(): pl.pallas_call(functools.partial(exchange_kernel, chunk, scaling), in_spe...]
    all_to_all x1 -> x0, blocking collectives: 178 us -> none  [on_device(): lax.all_to_all(spectra, 'chan', split_axis=2, concat_axis=3, tiled=True)]
    reduce_scatter x1 -> x0, waiting for transfers between devices: 61.9 us -> none  [on_device(): share = lax.psum_scatter(packed, 'range', scatter_dimension=0, tiled=True)]
    all_gather x1, waiting for transfers between devices: 34.6 us -> 49.3 us  [on_device(): factors = unpack_factor(lax.all_gather(mine, 'range', axis=0), count)]
    reshape x1 -> x0, local copies, waits for them, and re-layouts: 4.57 us -> none  [on_device(): spectra = spectra.reshape(2, tiles, pulses, channels, LANES)]
  transfers between devices with their start and end apart: 4 -> 2, of which waited for: 3 -> 1; matrix products, arithmetic and copies ran while one was open for 2% -> 2% of each run, Pallas kernels for 0% -> 0%
where the time goes in v2:
time: 397 us
  Pallas kernels  306 us (77%)
  waiting for transfers between devices  49.4 us (12%)
  local copies, waits for them, and re-layouts  18.1 us (5%)
  between operations  14.2 us (4%)
  other arithmetic  7.82 us (2%)
    pallas_call x1, Pallas kernels, exchange(): pl.pallas_call(functools.partial(exchange_kernel, chunk, scaling), in_spe...  233 us
    all_gather x1, waiting for transfers between devices, on_device(): factors = unpack_factor(lax.all_gather(mine, 'range', axis=0), count)  49.3 us
    pallas_call x1, Pallas kernels, make_spectra(): pl.pallas_call(functools.partial(spectra_kernel, channels, pulses, tiles,...  34.8 us
    pallas_call x1, Pallas kernels, make_factor(): pl.pallas_call(functools.partial(factor_kernel, count, order), out_shape=...  26.2 us
    pallas_call x1, Pallas kernels, unpack_factor(): pl.pallas_call(unpack_kernel, grid=(count, ranges), in_specs=[pl.BlockSpe...  11.6 us
  transfers between devices with their start and end apart: 2, of which 1 were waited for; matrix products, arithmetic and copies ran while one was open for 2% of the time, Pallas kernels for 0%

profile of v2, /device:TPU:0, one launch (start us, length us, event | category | flops | bytes accessed | tf_op | source)
XLA Modules:
  0.0 396.6 jit_solution(12963512584953225191)
XLA Ops:
  7.2 0.0 copy-start.2
  7.2 0.0 copy-start.1
  7.2 0.0 all-gather.3.cloned.1.call-start
  7.2 4.6 %slice.20 = f32[2,8,512,128]{3,2,1,0:T(8,128)} slice(f32[2,8,512,256]{3,2,1,0:T(8,128)} %e_ref.1), slice={[0:2], [0:8], [0:512], [0:128]} | slice | bytes 8388608 | tf_op jit(solution)/shard_map/slice | solution.py:447
  11.8 1.3 collective-permute-start
  13.1 0.0 copy-done.2
  13.1 0.7 copy.20.w_ref
  13.8 0.0 copy-done.1
  13.9 0.5 tile.10
  14.4 0.7 slice_reduce_fusion
  15.1 0.1 copy.19
  15.3 0.1 copy.18
  15.4 0.9 fusion.8
  16.3 4.2 %negate_multiply_fusion = (f32[512,512]{1,0:T(8,128)S(1)}, f32[512,512]{1,0:T(8,128)S(1)}) fusion(), kind=kLoop, calls=%fused_computation.12 | loop fusion | flops 4456448 | bytes 2097152 | tf_op jit(solution)/shard_map/mul | solution.py:62
  20.4 1.7 fusion
  22.1 0.0 collective-permute-done.h_ref
  22.1 34.8 %spectra.1 = f32[2,2,4104,128]{3,2,1,0:T(8,128)} custom-call(f32[2,8,512,256]{3,2,1,0:T(8,128)} %e_ref.1, f32[2,8,512,128]{3,2,1,0:T(8,128)} %collective-permute-done.h_ref, bf16[512,256]{1,0:T(8,128)(2,1)} %get-tuple-element.11.kh_ref, bf16[512,256]{1,0:T(8,128)(2,1)} %get-tuple-element.10.kl_ref, bf16[1024,512]{1,0:T(8,128)(2,1)} %get-tuple-element.9.th_ref, ...), custom_call_target="tpu_custom_call" | custom-call | tf_op jit(solution)/shard_map/spectra/pallas_call | solution.py:99
  56.9 233.3 %exchange.1 = (f32[16,128,128]{2,1,0:T(8,128)}, bf16[2,64,64,256]{3,2,1,0:T(8,128)(2,1)}) custom-call(f32[64,2]{1,0:T(8,128)} %copy.20.w_ref, f32[2,2,513,8,128]{4,3,2,1,0:T(8,128)} %bitcast.13), custom_call_target="tpu_custom_call" | custom-call | tf_op jit(solution)/shard_map/exchange/pallas_call | solution.py:308
  290.2 26.2 %factor.1 = f32[16,2,128,128]{3,2,1,0:T(8,128)} custom-call(f32[16,128,128]{2,1,0:T(8,128)} %get-tuple-element.5.z_ref), custom_call_target="tpu_custom_call" | custom-call | tf_op jit(solution)/shard_map/factor/pallas_call | solution.py:392
  316.4 0.0 copy-start
  316.4 2.4 slice.27
  318.8 1.6 copy.23
  320.4 0.0 copy-done
  320.4 1.1 fusion.4
  321.5 2.5 copy.22
  324.0 0.0 all-gather.3.cloned.1.call-update
  324.1 49.3 %all-gather.3.cloned.1.call-done = f32[64,128,128]{2,1,0:T(8,128)} async-done(((f32[16,128,128]{2,1,0:T(8,128)}), f32[64,128,128]{2,1,0:T(8,128)}) %all-gather.3.cloned.1.call-update) | async-done | bytes 4194320 | tf_op jit(solution)/shard_map/all_gather | solution.py:465
  373.4 11.6 %unpack.1 = f32[64,2,128,128]{3,2,1,0:T(8,128)} custom-call(f32[4,4,4,128,128]{4,3,2,1,0:T(8,128)} %bitcast.14), custom_call_target="tpu_custom_call" | custom-call | tf_op jit(solution)/shard_map/unpack/pallas_call | solution.py:426
  385.0 4.8 %copy.25 = bf16[2,64,64,256]{3,2,1,0:T(8,128)(2,1)} copy(bf16[2,64,64,256]{3,2,1,0:T(8,128)(2,1)} %get-tuple-element.16) | data formatting | bytes 8388608
  (7 shorter events, 0.1 us)
Async XLA Ops:
  7.2 6.0 %copy-start.2 = (s32[64,2]{0,1:T(2,128)S(1)}, s32[64,2]{0,1:T(2,128)}, u32[]{:S(2)}) copy-start(s32[64,2]{0,1:T(2,128)} %param.5) | copy-start | bytes 1540
  7.2 6.7 %copy-start.1 = (f32[2,129]{1,0:T(2,128)S(1)}, f32[2,129]{1,0:T(2,128)}, u32[]{:S(2)}) copy-start(f32[2,129]{1,0:T(2,128)} %param.4) | copy-start | bytes 3100
  7.2 366.2 %all-gather.3.cloned.1.call-start = ((), (), s32[]{:S(2)}) async-start(), calls=%async_computation | async-start | bytes 5242880 | tf_op jit(solution)/shard_map/all_gather | solution.py:465
  11.8 10.3 %collective-permute-start = (f32[2,8,512,128]{3,2,1,0:T(8,128)}, f32[2,8,512,128]{3,2,1,0:T(8,128)}, u32[]{:S(2)}, u32[]{:S(2)}) collective-permute-start(f32[2,8,512,128]{3,2,1,0:T(8,128)} %slice.20), channel_id=1, source_target_pairs={{8,0},{16,8},{24,16},{9,1},{17,9},{25,17},{10,2},{18,10},{26,18},{... | collective-permute-start | bytes 12582920 | tf_op jit(solution)/shard_map/ppermute | solution.py:41
  316.4 4.0 %copy-start = (f32[16,2,128,128]{3,2,1,0:T(8,128)S(1)}, f32[16,2,128,128]{3,2,1,0:T(8,128)}, u32[]{:S(2)}) copy-start(f32[16,2,128,128]{3,2,1,0:T(8,128)} %factor.1) | copy-start | bytes 6291460
Sparse Core Ops, SparseCore 0:
  324.2 49.1 all-gather.2

commit v3 on v2

--- a/solution.py
+++ b/solution.py
@@ -55,8 +55,9 @@
 
 
 def doppler_table(pulses):
-    bins = jnp.arange(pulses, dtype=jnp.int32)
-    phase = bins[:, None] * bins[None, :] % pulses
+    half = jnp.arange(pulses // 2, dtype=jnp.int32)
+    bins = jnp.concatenate([2 * half, 2 * half + 1])
+    phase = bins[:, None] * half[None, :] % pulses
     angles = phase.astype(F32) * (2.0 * math.pi / pulses)
     scaling = 1.0 / math.sqrt(pulses)
     return jnp.concatenate([jnp.cos(angles) * scaling, -jnp.sin(angles) * scaling])
@@ -70,12 +71,14 @@
         window = jnp.concatenate(
             [w[:, t * LANES : (t + 2) * LANES] for w in wide], -1
         )
-        y = split(dot3(split(window), kernel))
-        step = min(256, pulses)
-        for b in range(0, pulses, step):
-            re = dot3((th_ref[pl.ds(b, step), :], tl_ref[pl.ds(b, step), :]), y)
-            im = dot3((th_ref[pl.ds(pulses + b, step), :], tl_ref[pl.ds(pulses + b, step), :]), y)
-            rows = pl.ds(b * channels + channel, step, stride=channels)
+        y = dot3(split(window), kernel)
+        half = pulses // 2
+        folded = (split(y[:half] + y[half:]), split(y[:half] - y[half:]))
+        for b in range(2):
+            top, low = pl.ds(b * half, half), pl.ds((2 + b) * half, half)
+            re = dot3((th_ref[top, :], tl_ref[top, :]), folded[b])
+            im = dot3((th_ref[low, :], tl_ref[low, :]), folded[b])
+            rows = pl.ds(b * channels + channel, half, stride=2 * channels)
             real = re[:, :LANES] - im[:, LANES:]
             imag = re[:, LANES:] + im[:, :LANES]
             s_ref[0, t, rows, :] = real
@@ -170,7 +173,7 @@
 
 def exchange_kernel(
     chunk, scaling, w_ref, s_ref, share_ref, o_ref,
-    r_ref, z_ref, got_ref, own_sem, send_sem, recv_sem, zsend_sem, zrecv_sem,
+    r_ref, z_ref, got_ref, t_ref, own_sem, send_sem, recv_sem, zsend_sem, zrecv_sem,
 ):
     owners, ranges = lax.axis_size("chan"), lax.axis_size("range")
     me, here = lax.axis_index("chan"), lax.axis_index("range")
@@ -180,8 +183,13 @@
     count = total // chunk
     part = chunk // ranges
 
+    side = lax.rem(here, 2)
+
+    def target(k):
+        return lax.rem(me + k + side * (owners - 2 * k), owners)
+
     def chan_peer(k):
-        return {"chan": lax.rem(me + k, owners)}
+        return {"chan": target(k)}
 
     def range_peer(k):
         return {"range": lax.rem(here + k, ranges)}
@@ -204,7 +212,7 @@
 
     def outgoing(c, k):
         start, size = span(c)
-        owner = lax.rem(me + k, owners)
+        owner = target(k)
         return pltpu.make_async_remote_copy(
             src_ref=s_ref.at[:, :, pl.ds(owner * total + start, size)],
             dst_ref=r_ref.at[:, :, pl.ds(start, size), mine],
@@ -222,14 +230,18 @@
             own_sem.at[c],
         )
 
+    twin = here + 1 - 2 * lax.rem(here, 2)
+    over = lax.rem(here + 2, ranges)
+    far = lax.rem(twin + 2, ranges)
+
     def summand(c, k):
-        target = lax.rem(here + k, ranges)
+        source = z_ref.at[pl.ds(c * chunk + (twin, far)[k] * part, part)] if k < 2 else t_ref.at[c]
         return pltpu.make_async_remote_copy(
-            src_ref=z_ref.at[pl.ds(c * chunk + target * part, part)],
-            dst_ref=got_ref.at[c, k - 1],
-            send_sem=zsend_sem.at[c, k - 1],
-            recv_sem=zrecv_sem.at[c, k - 1],
-            device_id=range_peer(k),
+            src_ref=source,
+            dst_ref=got_ref.at[c, k],
+            send_sem=zsend_sem.at[c, k],
+            recv_sem=zrecv_sem.at[c, k],
+            device_id={"range": twin if k < 2 else over},
             device_id_type=pl.DeviceIdType.MESH,
         )
 
@@ -242,16 +254,19 @@
     cols = lax.broadcasted_iota(jnp.int32, (order, order), 1)
     upper = rows <= cols
 
+    def relay(c):
+        summand(c, 1).wait_recv()
+        t_ref[c] = z_ref[pl.ds(c * chunk + over * part, part)] + got_ref[c, 1]
+        summand(c, 0).wait_recv()
+        share_ref[pl.ds(c * part, part)] = (
+            z_ref[pl.ds(c * chunk + here * part, part)] + got_ref[c, 0]
+        )
+        summand(c, 2).start()
+
     def collect(c):
-        for k in range(1, ranges):
-            summand(c, k).wait_recv()
-
-        @pl.loop(0, part)
-        def _(j):
-            value = z_ref[c * chunk + here * part + j]
-            for k in range(1, ranges):
-                value = value + got_ref[c, k - 1, j]
-            share_ref[c * part + j] = value
+        summand(c, 2).wait_recv()
+        span = pl.ds(c * part, part)
+        share_ref[span] = share_ref[span] + got_ref[c, 2]
 
     for c in range(count):
         for k in range(1, owners):
@@ -285,15 +300,19 @@
                 for t in range(tiles):
                     o_ref[p, j, :, t * LANES : (t + 1) * LANES] = r_ref[p, t, j].astype(BF)
 
-        for k in range(1, ranges):
-            summand(c, k).start()
+        for k in range(2):
+            summand(c, 1 - k).start()
         if c > 0:
-            collect(c - 1)
-    collect(count - 1)
+            relay(c - 1)
+        if c > 1:
+            collect(c - 2)
+    relay(count - 1)
+    for c in range(max(0, count - 2), count):
+        collect(c)
     for c in range(count):
         for k in range(1, owners):
             outgoing(c, k).wait_send()
-        for k in range(1, ranges):
+        for k in range(3):
             summand(c, k).wait_send()
 
 
@@ -319,12 +338,13 @@
         scratch_shapes=[
             pltpu.VMEM((2, tiles, total + 1, full, LANES), F32),
             pltpu.VMEM((total, order, order), F32),
-            pltpu.VMEM((count, ranges - 1, part, order, order), F32),
+            pltpu.VMEM((count, 3, part, order, order), F32),
+            pltpu.VMEM((count, part, order, order), F32),
             dma((count,)),
             dma((count, owners - 1)),
             dma((count, owners - 1)),
-            dma((count, ranges - 1)),
-            dma((count, ranges - 1)),
+            dma((count, 3)),
+            dma((count, 3)),
         ],
         compiler_params=pltpu.CompilerParams(
             vmem_limit_bytes=VMEM_LIMIT, collective_id=0, has_side_effects=True
@@ -369,8 +389,8 @@
         for b in range(count):
             fr = sr_ref[pl.ds(b, STRIP, stride=count), :]
             fi = si_ref[pl.ds(b, STRIP, stride=count), :]
-            o_ref[b, 0, offset:done, :] = fr
-            o_ref[b, 1, offset:done, :] = fi
+            re_ref[b, offset:done, :] = fr
+            im_ref[b, offset:done, :] = fi
             if done < order:
                 left = jnp.concatenate([fr, fi], 0)
                 right = jnp.concatenate(
@@ -386,12 +406,16 @@
                 re_ref[b, done:, :] = re_ref[b, done:, :] - update[done:, :order]
                 im_ref[b, done:, :] = im_ref[b, done:, :] - update[done:, order:]
 
+    @pl.loop(0, count)
+    def _(b):
+        o_ref[b] = jnp.where(rows <= cols, re_ref[b], im_ref[b].T)
+
 
 def make_factor(gram):
     count, order, _ = gram.shape
     return pl.pallas_call(
         functools.partial(factor_kernel, count, order),
-        out_shape=jax.ShapeDtypeStruct((count, 2, order, order), F32),
+        out_shape=jax.ShapeDtypeStruct((count, order, order), F32),
         scratch_shapes=[
             pltpu.VMEM((count, order, order), F32),
             pltpu.VMEM((count, order, order), F32),
@@ -403,10 +427,59 @@
     )(gram)
 
 
-def pack_factor(factors):
-    order = factors.shape[-1]
-    keep = jnp.arange(order)[:, None] <= jnp.arange(order)[None, :]
-    return jnp.where(keep, factors[:, 0], jnp.swapaxes(factors[:, 1], 1, 2))
+def gather_kernel(pieces, p_ref, o_ref, own_sem, send_sem, recv_sem):
+    here = lax.axis_index("range")
+    twin = here + 1 - 2 * lax.rem(here, 2)
+    over = lax.rem(here + 2, 4)
+    size = p_ref.shape[0] // pieces
+
+    barrier = pltpu.get_barrier_semaphore()
+    for peer in (twin, over):
+        pl.semaphore_signal(
+            barrier, inc=1, device_id={"range": peer}, device_id_type=pl.DeviceIdType.MESH
+        )
+    pl.semaphore_wait(barrier, 2)
+
+    def send(kind, q):
+        span = pl.ds(q * size, size)
+        owner, peer = ((here, over), (here, twin), (over, twin))[kind]
+        return pltpu.make_async_remote_copy(
+            src_ref=p_ref.at[span] if kind < 2 else o_ref.at[owner, span],
+            dst_ref=o_ref.at[owner, span],
+            send_sem=send_sem.at[kind, q],
+            recv_sem=recv_sem.at[kind, q],
+            device_id={"range": peer},
+            device_id_type=pl.DeviceIdType.MESH,
+        )
+
+    for kind in range(2):
+        for q in range(pieces):
+            send(kind, q).start()
+    own = pltpu.make_async_copy(p_ref, o_ref.at[here], own_sem)
+    own.start()
+    for q in range(pieces):
+        send(0, q).wait_recv()
+        send(2, q).start()
+    for q in range(pieces):
+        send(1, q).wait_recv()
+        send(2, q).wait_recv()
+        for kind in range(3):
+            send(kind, q).wait_send()
+    own.wait()
+
+
+def gather(packed):
+    pieces = math.gcd(packed.shape[0], 4)
+    dma = pltpu.SemaphoreType.DMA
+    return pl.pallas_call(
+        functools.partial(gather_kernel, pieces),
+        in_specs=[pl.BlockSpec(memory_space=pltpu.VMEM)],
+        out_specs=pl.BlockSpec(memory_space=pl.ANY),
+        out_shape=jax.ShapeDtypeStruct((4,) + packed.shape, F32),
+        scratch_shapes=[dma, dma((3, pieces)), dma((3, pieces))],
+        compiler_params=pltpu.CompilerParams(collective_id=1, has_side_effects=True),
+        name="gather",
+    )(packed)
 
 
 def unpack_kernel(p_ref, o_ref):
@@ -447,7 +520,7 @@
     rim = from_behind(echoes[..., :tap_span], "range", -1)
     weights = train_mask.astype(F32)
     scaling = 1.0 / (gates * ranges)
-    wrap = int(channels % 8 == 0 and chunk % ranges == 0)
+    wrap = int(channels % 8 == 0 and chunk % ranges == 0 and ranges == 4)
     spectra = make_spectra(echoes, rim, chirp, wrap)
     spectra = spectra.reshape(2, tiles, pulses + wrap, channels, LANES)
     if wrap:
@@ -461,8 +534,9 @@
         firsts = jnp.concatenate([turned[:, :, bins::bins], edge], 2)
         packed, spectra_out = make_gram(turned, firsts, weights, scaling, bins)
         share = lax.psum_scatter(packed, "range", scatter_dimension=0, tiled=True)
-    mine = pack_factor(make_factor(share))
-    factors = unpack_factor(lax.all_gather(mine, "range", axis=0), count)
+    mine = make_factor(share)
+    pooled = gather(mine) if ranges == 4 else lax.all_gather(mine, "range", axis=0)
+    factors = unpack_factor(pooled, count)
     return (spectra_out, factors)
 
 

time: 397 us -> 366 us (0.922)
  waiting for transfers between devices: 49.4 us -> 1.62 us
  Pallas kernels: 306 us -> 346 us
  between operations: 14.2 us -> 0.76 us
  local copies, waits for them, and re-layouts: 18.1 us -> 11.6 us
    all_gather x1 -> x0, waiting for transfers between devices: 49.3 us -> none  [on_device(): factors = unpack_factor(lax.all_gather(mine, 'range', axis=0), count)]
    pallas_call x0 -> x1, Pallas kernels: none -> 28.7 us  [gather(): pl.pallas_call(functools.partial(gather_kernel, pieces), in_specs=[pl.Blo...]
    pallas_call x1, Pallas kernels: 233 us -> 248 us  [exchange(): pl.pallas_call(functools.partial(exchange_kernel, chunk, scaling), in_spe...]
    pallas_call x1, Pallas kernels: 34.8 us -> 29.6 us  [make_spectra(): pl.pallas_call(functools.partial(spectra_kernel, channels, pulses, tiles,...]
  transfers between devices with their start and end apart: 2 -> 1, of which waited for: 1 -> 1; matrix products, arithmetic and copies ran while one was open for 2% -> 2% of each run, Pallas kernels for 0% -> 0%
where the time goes in v3:
time: 366 us; the launch traced here: 365 us
  Pallas kernels  346 us (95%)
  local copies, waits for them, and re-layouts  11.6 us (3%)
  other arithmetic  4.21 us (1%)
    pallas_call x1, Pallas kernels, exchange(): pl.pallas_call(functools.partial(exchange_kernel, chunk, scaling), in_spe...  248 us
    pallas_call x1, Pallas kernels, make_spectra(): pl.pallas_call(functools.partial(spectra_kernel, channels, pulses, tiles,...  29.6 us
    pallas_call x1, Pallas kernels, gather(): pl.pallas_call(functools.partial(gather_kernel, pieces), in_specs=[pl.Blo...  28.7 us
    pallas_call x1, Pallas kernels, make_factor(): pl.pallas_call(functools.partial(factor_kernel, count, order), out_shape=...  27.4 us
    pallas_call x1, Pallas kernels, unpack_factor(): pl.pallas_call(unpack_kernel, grid=(count, ranges), in_specs=[pl.BlockSpe...  11.6 us
  transfers between devices with their start and end apart: 1, of which 1 were waited for; matrix products, arithmetic and copies ran while one was open for 2% of the time, Pallas kernels for 0%

profile of v3, /device:TPU:0, one launch (start us, length us, event | category | flops | bytes accessed | tf_op | source)
XLA Modules:
  0.0 365.3 jit_solution(16860710200785743417)
XLA Ops:
  0.6 0.0 copy-start.1
  0.6 0.0 copy-start
  0.6 4.6 %slice.14 = f32[2,8,512,128]{3,2,1,0:T(8,128)} slice(f32[2,8,512,256]{3,2,1,0:T(8,128)} %e_ref.1), slice={[0:2], [0:8], [0:512], [0:128]} | slice | bytes 8388608 | tf_op jit(solution)/shard_map/slice | solution.py:520
  5.3 1.3 collective-permute-start
  6.6 0.0 copy-done.1
  6.6 0.7 copy.11.w_ref
  7.3 0.0 copy-done
  7.3 0.5 tile.10
  7.8 0.7 slice_reduce_fusion
  8.6 0.1 copy.10
  8.7 0.1 copy.9
  8.8 0.9 fusion.1
  9.8 2.2 cosine_multiply_fusion
  11.9 1.1 fusion
  13.0 1.6 collective-permute-done.h_ref
  14.7 29.6 %spectra.1 = f32[2,2,4104,128]{3,2,1,0:T(8,128)} custom-call(f32[2,8,512,256]{3,2,1,0:T(8,128)} %e_ref.1, f32[2,8,512,128]{3,2,1,0:T(8,128)} %collective-permute-done.h_ref, bf16[512,256]{1,0:T(8,128)(2,1)} %get-tuple-element.11.kh_ref, bf16[512,256]{1,0:T(8,128)(2,1)} %get-tuple-element.10.kl_ref, bf16[1024,256]{1,0:T(8,128)(2,1)} %get-tuple-element.9.th_ref, ...), custom_call_target="tpu_custom_call" | custom-call | tf_op jit(solution)/shard_map/spectra/pallas_call | solution.py:102
  44.3 248.4 %exchange.1 = (f32[16,128,128]{2,1,0:T(8,128)}, bf16[2,64,64,256]{3,2,1,0:T(8,128)(2,1)}) custom-call(f32[64,2]{1,0:T(8,128)} %copy.11.w_ref, f32[2,2,513,8,128]{4,3,2,1,0:T(8,128)} %bitcast.5), custom_call_target="tpu_custom_call" | custom-call | tf_op jit(solution)/shard_map/exchange/pallas_call | solution.py:327
  292.7 27.4 %factor.1.p_ref = f32[16,128,128]{2,1,0:T(8,128)} custom-call(f32[16,128,128]{2,1,0:T(8,128)} %get-tuple-element.5.z_ref), custom_call_target="tpu_custom_call" | custom-call | tf_op jit(solution)/shard_map/factor/pallas_call | solution.py:416
  320.1 28.7 %gather.1 = f32[4,16,128,128]{3,2,1,0:T(8,128)} custom-call(f32[16,128,128]{2,1,0:T(8,128)} %factor.1.p_ref), custom_call_target="tpu_custom_call" | custom-call | tf_op jit(solution)/shard_map/gather/pallas_call | solution.py:474
  348.9 11.6 %unpack.1 = f32[64,2,128,128]{3,2,1,0:T(8,128)} custom-call(f32[4,4,4,128,128]{4,3,2,1,0:T(8,128)} %bitcast.6), custom_call_target="tpu_custom_call" | custom-call | tf_op jit(solution)/shard_map/unpack/pallas_call | solution.py:499
  360.5 4.8 %copy.13 = bf16[2,64,64,256]{3,2,1,0:T(8,128)(2,1)} copy(bf16[2,64,64,256]{3,2,1,0:T(8,128)(2,1)} %get-tuple-element.18) | data formatting | bytes 8388608
  (8 shorter events, 0.1 us)
Async XLA Ops:
  0.6 5.9 %copy-start.1 = (s32[64,2]{0,1:T(2,128)S(1)}, s32[64,2]{0,1:T(2,128)}, u32[]{:S(2)}) copy-start(s32[64,2]{0,1:T(2,128)} %param.5) | copy-start | bytes 1540
  0.6 6.6 %copy-start = (f32[2,129]{1,0:T(2,128)S(1)}, f32[2,129]{1,0:T(2,128)}, u32[]{:S(2)}) copy-start(f32[2,129]{1,0:T(2,128)} %param.4) | copy-start | bytes 3100
  5.3 9.4 %collective-permute-start = (f32[2,8,512,128]{3,2,1,0:T(8,128)}, f32[2,8,512,128]{3,2,1,0:T(8,128)}, u32[]{:S(2)}, u32[]{:S(2)}) collective-permute-start(f32[2,8,512,128]{3,2,1,0:T(8,128)} %slice.14), channel_id=1, source_target_pairs={{8,0},{16,8},{24,16},{9,1},{17,9},{25,17},{10,2},{18,10},{26,18},{... | collective-permute-start | bytes 12582920 | tf_op jit(solution)/shard_map/ppermute | solution.py:41

commit v4 on v3

--- a/solution.py
+++ b/solution.py
@@ -183,10 +183,13 @@
     count = total // chunk
     part = chunk // ranges
 
-    side = lax.rem(here, 2)
+    group = owners // 2
+    half, place = me // group, lax.rem(me, group)
 
     def target(k):
-        return lax.rem(me + k + side * (owners - 2 * k), owners)
+        if k < group:
+            return half * group + lax.rem(place + k, group)
+        return (1 - half) * group + lax.rem(place + k, group)
 
     def chan_peer(k):
         return {"chan": target(k)}
@@ -245,9 +248,11 @@
             device_id_type=pl.DeviceIdType.MESH,
         )
 
+    for reach in (range(1, group), range(group, owners)):
+        for c in range(count):
+            for k in reach:
+                outgoing(c, k).start()
     for c in range(count):
-        for k in range(1, owners):
-            outgoing(c, k).start()
         local(c).start()
 
     rows = lax.broadcasted_iota(jnp.int32, (order, order), 0)

time: 366 us -> 374 us (1.022)
  Pallas kernels: 346 us -> 354 us
    pallas_call x1, Pallas kernels: 248 us -> 256 us  [exchange(): pl.pallas_call(functools.partial(exchange_kernel, chunk, scaling), in_spe...]
where the time goes in v4:
time: 374 us
  Pallas kernels  354 us (95%)
  local copies, waits for them, and re-layouts  11.6 us (3%)
  other arithmetic  4.21 us (1%)
    pallas_call x1, Pallas kernels, exchange(): pl.pallas_call(functools.partial(exchange_kernel, chunk, scaling), in_spe...  256 us
    pallas_call x1, Pallas kernels, make_spectra(): pl.pallas_call(functools.partial(spectra_kernel, channels, pulses, tiles,...  29.6 us
    pallas_call x1, Pallas kernels, gather(): pl.pallas_call(functools.partial(gather_kernel, pieces), in_specs=[pl.Blo...  29.5 us
    pallas_call x1, Pallas kernels, make_factor(): pl.pallas_call(functools.partial(factor_kernel, count, order), out_shape=...  27.4 us
    pallas_call x1, Pallas kernels, unpack_factor(): pl.pallas_call(unpack_kernel, grid=(count, ranges), in_specs=[pl.BlockSpe...  11.6 us
  transfers between devices with their start and end apart: 1, of which 1 were waited for; matrix products, arithmetic and copies ran while one was open for 2% of the time, Pallas kernels for 0%

profile of v4, /device:TPU:0, one launch (start us, length us, event | category | flops | bytes accessed | tf_op | source)
XLA Modules:
  0.0 373.7 jit_solution(3743324840998365850)
XLA Ops:
  0.6 0.0 copy-start.1
  0.6 0.0 copy-start
  0.6 4.6 %slice.14 = f32[2,8,512,128]{3,2,1,0:T(8,128)} slice(f32[2,8,512,256]{3,2,1,0:T(8,128)} %e_ref.1), slice={[0:2], [0:8], [0:512], [0:128]} | slice | bytes 8388608 | tf_op jit(solution)/shard_map/slice | solution.py:525
  5.3 1.3 collective-permute-start
  6.6 0.0 copy-done.1
  6.6 0.7 copy.11.w_ref
  7.3 0.0 copy-done
  7.3 0.5 tile.10
  7.8 0.7 slice_reduce_fusion
  8.6 0.1 copy.10
  8.7 0.1 copy.9
  8.8 0.9 fusion.1
  9.8 2.2 cosine_multiply_fusion
  11.9 1.1 fusion
  13.0 1.6 collective-permute-done.h_ref
  14.7 29.6 %spectra.1 = f32[2,2,4104,128]{3,2,1,0:T(8,128)} custom-call(f32[2,8,512,256]{3,2,1,0:T(8,128)} %e_ref.1, f32[2,8,512,128]{3,2,1,0:T(8,128)} %collective-permute-done.h_ref, bf16[512,256]{1,0:T(8,128)(2,1)} %get-tuple-element.11.kh_ref, bf16[512,256]{1,0:T(8,128)(2,1)} %get-tuple-element.10.kl_ref, bf16[1024,256]{1,0:T(8,128)(2,1)} %get-tuple-element.9.th_ref, ...), custom_call_target="tpu_custom_call" | custom-call | tf_op jit(solution)/shard_map/spectra/pallas_call | solution.py:102
  44.3 256.1 %exchange.1 = (f32[16,128,128]{2,1,0:T(8,128)}, bf16[2,64,64,256]{3,2,1,0:T(8,128)(2,1)}) custom-call(f32[64,2]{1,0:T(8,128)} %copy.11.w_ref, f32[2,2,513,8,128]{4,3,2,1,0:T(8,128)} %bitcast.5), custom_call_target="tpu_custom_call" | custom-call | tf_op jit(solution)/shard_map/exchange/pallas_call | solution.py:332
  300.4 27.4 %factor.1.p_ref = f32[16,128,128]{2,1,0:T(8,128)} custom-call(f32[16,128,128]{2,1,0:T(8,128)} %get-tuple-element.5.z_ref), custom_call_target="tpu_custom_call" | custom-call | tf_op jit(solution)/shard_map/factor/pallas_call | solution.py:421
  327.9 29.5 %gather.1 = f32[4,16,128,128]{3,2,1,0:T(8,128)} custom-call(f32[16,128,128]{2,1,0:T(8,128)} %factor.1.p_ref), custom_call_target="tpu_custom_call" | custom-call | tf_op jit(solution)/shard_map/gather/pallas_call | solution.py:479
  357.3 11.6 %unpack.1 = f32[64,2,128,128]{3,2,1,0:T(8,128)} custom-call(f32[4,4,4,128,128]{4,3,2,1,0:T(8,128)} %bitcast.6), custom_call_target="tpu_custom_call" | custom-call | tf_op jit(solution)/shard_map/unpack/pallas_call | solution.py:504
  369.0 4.8 %copy.13 = bf16[2,64,64,256]{3,2,1,0:T(8,128)(2,1)} copy(bf16[2,64,64,256]{3,2,1,0:T(8,128)(2,1)} %get-tuple-element.18) | data formatting | bytes 8388608
  (8 shorter events, 0.1 us)
Async XLA Ops:
  0.6 5.9 %copy-start.1 = (s32[64,2]{0,1:T(2,128)S(1)}, s32[64,2]{0,1:T(2,128)}, u32[]{:S(2)}) copy-start(s32[64,2]{0,1:T(2,128)} %param.5) | copy-start | bytes 1540
  0.6 6.6 %copy-start = (f32[2,129]{1,0:T(2,128)S(1)}, f32[2,129]{1,0:T(2,128)}, u32[]{:S(2)}) copy-start(f32[2,129]{1,0:T(2,128)} %param.4) | copy-start | bytes 3100
  5.3 9.4 %collective-permute-start = (f32[2,8,512,128]{3,2,1,0:T(8,128)}, f32[2,8,512,128]{3,2,1,0:T(8,128)}, u32[]{:S(2)}, u32[]{:S(2)}) collective-permute-start(f32[2,8,512,128]{3,2,1,0:T(8,128)} %slice.14), channel_id=1, source_target_pairs={{8,0},{16,8},{24,16},{9,1},{17,9},{25,17},{10,2},{18,10},{26,18},{... | collective-permute-start | bytes 12582920 | tf_op jit(solution)/shard_map/ppermute | solution.py:41
